TPU v7x, 32 devices: a whole 2x2x4 slice. The times are simulated.
32 devices in a mesh: groups: 2 (over x), req: 16 (over z, y, core).
Axes of the slice: x: 2, y: 2, z: 4, core: 2. Of those that a mesh axis runs over, the one named last changes fastest.
Arguments:
- queries: bfloat16 [2, 2048, 512], P(None, ('groups', 'req')), parts along dimension 1, may hold values from -40 to 40
- new_kv: bfloat16 [2, 2048, 128], P(None, ('groups', 'req')), parts along dimension 1, may hold values from -4 to 4
- cache: bfloat16 [2, 2048, 128, 128], P(None, ('groups', 'req')), parts along dimension 1, may hold values from -4 to 4
- lengths: int32 [2, 256], P(None, 'groups'), parts along dimension 1, may hold values from 2 to 128
- residual: bfloat16 [2, 256, 2880], P(None, ('groups', 'req')), parts along dimension 1, may hold values from -30 to 30
- o_proj: bfloat16 [4096, 2880], P('req'), may hold values from -1 to 1
- router: bfloat16 [2880, 16], replicated, may hold values from -0.109375 to 0.109375
- w_gate: bfloat16 [64, 2880, 360], P('req'), may hold values from -0.109375 to 0.109375
- w_up: bfloat16 [64, 2880, 360], P('req'), may hold values from -0.109375 to 0.109375
- w_down: bfloat16 [64, 360, 2880], P('req'), may hold values from -0.15625 to 0.15625
- routes: int32 [2, 256, 4], P(None, ('groups', 'req')), parts along dimension 1, may hold values from 0 to 15, all different within a row; in each aligned block of 8 rows (0 to 7, 8 to 15, ..., all dimensions but the last counted through in order) at most 4 rows name the same one
Outputs:
- attended: bfloat16 [2, 256, 2880], P(None, ('groups', 'req')), parts along dimension 1
- layer_out: bfloat16 [2, 256, 2880], P(None, ('groups', 'req')), parts along dimension 1
There are 2 independent parts, one for each index of `groups`. A program takes and returns all parts, laid end to end along the dimension named above; an argument that names none is the same for every part. Nothing has to cross between parts.
Inputs may be any that keep to these rules, and one draw needn't show every extreme that they name: `routes`: each row names 4 different experts; of the 8 rows of one device of one micro-batch at most 4 name any one expert, and in every draw some expert is named by exactly 4 rows of some device.
All inputs are finite; a program needn't handle non-finite values.
Results may differ from a plain program's by a relative error of at most 0.0075.
Values may be sent and summed in bfloat16 or wider, within the bound.
A program may use at most 128 MiB of HBM per device.

v0:
```python
import math

import jax
import jax.numpy as jnp
from jax import lax
from jax.sharding import PartitionSpec as P

D = 2880
HD = 64
KVH = 8
QPK = 8
WIN = 128
EXPERTS = 16
SPLIT = 4
TOPK = 4
MB = 2
REQ_DEV = 8
FFS = 360
CAP = 4


def from_partner(value, axis, stride):
    mask = 2**stride
    pairs = [(source, source ^ mask) for source in range(lax.axis_size(axis))]
    return lax.ppermute(value, axis, pairs)


def attention_rows(query_rows, new_pair, cache_rows, live_count):
    row_total = query_rows.shape[0]
    query_heads = query_rows.reshape(row_total, QPK, HD)
    factor = 1.0 / math.sqrt(HD)
    scores = (
        jnp.einsum(
            "rqd,rpd->rqp", query_heads, cache_rows[:, :, :HD], preferred_element_type=jnp.float32
        )
        * factor
    )
    own_score = (
        jnp.einsum("rqd,rd->rq", query_heads, new_pair[:, :HD], preferred_element_type=jnp.float32)
        * factor
    )
    live = jnp.arange(WIN)[None, None, :] < live_count[:, None, None]
    masked = jnp.where(live, scores, -jnp.inf)
    top_score = jnp.maximum(jnp.max(masked, axis=2), own_score)
    weight_cached = jnp.exp(masked - top_score[:, :, None])
    weight_own = jnp.exp(own_score - top_score)
    total = jnp.sum(weight_cached, axis=2) + weight_own
    prob_cached = (weight_cached / total[:, :, None]).astype(jnp.bfloat16)
    prob_own = (weight_own / total).astype(jnp.bfloat16)
    mixed = jnp.einsum(
        "rqp,rpd->rqd", prob_cached, cache_rows[:, :, HD:], preferred_element_type=jnp.float32
    )
    mixed = (
        mixed
        + prob_own.astype(jnp.float32)[:, :, None]
        * new_pair[:, HD:].astype(jnp.float32)[:, None, :]
    )
    return mixed.astype(jnp.bfloat16)


def bit_value(device_index, bit_number):
    return device_index // (1 << bit_number) % 2


def expert_grouped(buffer, w_gate, w_up, w_down, device_count, device_index):
    batch_width = buffer.shape[0]
    spread = max(1, device_count // EXPERTS)
    experts_local = max(1, EXPERTS // device_count)
    quarters_local = SPLIT // spread
    piece_rows = CAP // spread
    sent = buffer.reshape(batch_width, EXPERTS * spread, piece_rows, D)
    arrived = lax.all_to_all(sent, "req", split_axis=1, concat_axis=2, tiled=True)
    spread_levels = spread.bit_length() - 1
    for section_bit in range(spread_levels):
        upper = bit_value(device_index, section_bit) == 1
        received = from_partner(arrived, "req", section_bit)
        arrived = jnp.where(
            upper,
            jnp.concatenate([received, arrived], axis=2),
            jnp.concatenate([arrived, received], axis=2),
        )
    gate_local = w_gate.reshape(experts_local, quarters_local, D, FFS)
    up_local = w_up.reshape(experts_local, quarters_local, D, FFS)
    down_local = w_down.reshape(experts_local, quarters_local, FFS, D)
    gate_hidden = jnp.einsum(
        "merd,eqdf->meqrf", arrived, gate_local, preferred_element_type=jnp.float32
    )
    up_hidden = jnp.einsum(
        "merd,eqdf->meqrf", arrived, up_local, preferred_element_type=jnp.float32
    )
    active = ((up_hidden + 1.0) * gate_hidden * jax.nn.sigmoid(1.702 * gate_hidden)).astype(
        jnp.bfloat16
    )
    partial_out = jnp.einsum(
        "meqrf,eqfd->merd", active, down_local, preferred_element_type=jnp.float32
    )
    for section_bit in reversed(range(spread_levels)):
        upper = bit_value(device_index, section_bit) == 1
        halves = partial_out.reshape(batch_width, experts_local, 2, partial_out.shape[2] // 2, D)
        keep_part = jnp.where(upper, halves[:, :, 1], halves[:, :, 0])
        send_part = jnp.where(upper, halves[:, :, 0], halves[:, :, 1])
        received = from_partner(send_part.astype(jnp.bfloat16), "req", section_bit).astype(
            send_part.dtype
        )
        partial_out = keep_part + received
    came_back = lax.all_to_all(
        partial_out.astype(jnp.bfloat16), "req", split_axis=2, concat_axis=1, tiled=True
    ).astype(partial_out.dtype)
    return came_back.reshape(batch_width, EXPERTS * CAP, D)


def shards(queries, new_kv, cache, lengths, residual, o_proj, router, w_gate, w_up, w_down, routes):
    device_count = lax.axis_size("req")
    device_index = lax.axis_index("req")
    group_size = device_count // KVH
    group_bits = group_size.bit_length() - 1
    local_rows = queries.shape[1]
    request_count = local_rows * group_size
    block_index = device_index % group_size
    local_lengths = lax.dynamic_slice_in_dim(lengths, block_index * local_rows, local_rows, 1)

    def process_batches(first_batch, batch_width):
        query_part = queries[first_batch : first_batch + batch_width].reshape(
            batch_width * local_rows, QPK * HD
        )
        pair_part = new_kv[first_batch : first_batch + batch_width].reshape(
            batch_width * local_rows, 2 * HD
        )
        cache_part = cache[first_batch : first_batch + batch_width].reshape(
            batch_width * local_rows, WIN, 2 * HD
        )
        live_part = local_lengths[first_batch : first_batch + batch_width].reshape(
            batch_width * local_rows
        )
        mixed = attention_rows(query_part, pair_part, cache_part, live_part)
        held = mixed.reshape(batch_width, local_rows, group_size, QPK // group_size * HD)
        for section_bit in range(group_bits):
            upper = bit_value(device_index, section_bit) == 1
            paired = held.reshape(batch_width, held.shape[1], held.shape[2] // 2, 2, held.shape[3])
            keep_part = jnp.where(upper, paired[:, :, :, 1], paired[:, :, :, 0])
            send_part = jnp.where(upper, paired[:, :, :, 0], paired[:, :, :, 1])
            received = from_partner(send_part, "req", section_bit)
            held = jnp.where(
                upper,
                jnp.concatenate([received, keep_part], axis=1),
                jnp.concatenate([keep_part, received], axis=1),
            )
        head_rows = held.reshape(batch_width, request_count, held.shape[3]).transpose(1, 0, 2)
        summed = lax.psum_scatter(
            jnp.einsum("rmk,kd->rmd", head_rows, o_proj, preferred_element_type=jnp.float32),
            "req",
            scatter_dimension=0,
            tiled=True,
        )
        attended_wide = residual[first_batch : first_batch + batch_width].astype(
            jnp.float32
        ) + summed.transpose(1, 0, 2)
        attended = attended_wide.astype(jnp.bfloat16)
        attended_wide = attended.astype(jnp.float32)
        normed = (
            attended_wide
            * lax.rsqrt(jnp.mean(attended_wide * attended_wide, axis=2, keepdims=True) + 1e-05)
        ).astype(jnp.bfloat16)
        logits = jnp.einsum("mrd,de->mre", normed, router, preferred_element_type=jnp.float32)
        route_ids = routes[first_batch : first_batch + batch_width]
        chosen = jnp.take_along_axis(logits, route_ids, axis=2)
        gates = 1.0 / jnp.sum(jnp.exp(chosen[:, :, None, :] - chosen[:, :, :, None]), axis=3)
        one_hot = (
            route_ids.reshape(batch_width, REQ_DEV * TOPK)[:, :, None]
            == jnp.arange(EXPERTS, dtype=jnp.int32)[None, None, :]
        ).astype(jnp.int32)
        earlier = jnp.cumsum(one_hot, axis=1) - one_hot
        ranks = jnp.sum(earlier * one_hot, axis=2).reshape(batch_width, REQ_DEV, TOPK)
        batch_offset = (jnp.arange(batch_width, dtype=jnp.int32) * (EXPERTS * CAP))[:, None, None]
        flat_index = batch_offset + route_ids * CAP + ranks
        repeated = jnp.repeat(normed.reshape(batch_width * REQ_DEV, D), TOPK, axis=0)
        buffer = (
            jnp.zeros((batch_width * EXPERTS * CAP, D), jnp.bfloat16)
            .at[flat_index.reshape(-1)]
            .set(repeated)
        )
        buffer = buffer.reshape(batch_width, EXPERTS, CAP, D)
        returned = expert_grouped(buffer, w_gate, w_up, w_down, device_count, device_index)
        picked = jnp.take(returned.reshape(batch_width * EXPERTS * CAP, D), flat_index, axis=0)
        mixture = jnp.sum(gates[:, :, :, None] * picked, axis=2)
        layer = (attended_wide + mixture).astype(jnp.bfloat16)
        return (attended, layer)

    results = [process_batches(batch_index, 1) for batch_index in range(MB)]
    attended_all = jnp.concatenate([result[0] for result in results], axis=0)
    layer_all = jnp.concatenate([result[1] for result in results], axis=0)
    return (attended_all, layer_all)


def solution(mesh):
    placed = (
        P(None, ("groups", "req"), None),
        P(None, ("groups", "req"), None),
        P(None, ("groups", "req"), None, None),
        P(None, "groups"),
        P(None, ("groups", "req"), None),
        P("req", None),
        P(),
        P("req", None, None),
        P("req", None, None),
        P("req", None, None),
        P(None, ("groups", "req"), None),
    )
    return jax.shard_map(
        shards,
        mesh=mesh,
        in_specs=placed,
        out_specs=(P(None, ("groups", "req"), None), P(None, ("groups", "req"), None)),
        check_vma=False,
    )
```

profile of v0, /device:TPU:0, one launch (start us, length us, event | category | flops | bytes accessed | tf_op | source)
XLA Modules:
  0.0 243.5 jit_solution(3754402669353376935)
XLA Ops:
  7.2 4.8 %fusion.88 = (bf16[1,64,128,128]{3,2,1,0:T(8,128)(2,1)}, bf16[1,64,128,128]{3,2,1,0:T(8,128)(2,1)}) fusion(bf16[2,64,128,128]{3,2,1,0:T(8,128)(2,1)} %param.17), kind=kLoop, calls=%fused_computation.172 | loop fusion | bytes 8388608 | tf_op jit(solution)/shard_map/slice | solution.py:129
  12.1 4.1 %copy.162 = bf16[1,64,128,128]{2,3,1,0:T(8,128)(2,1)} copy(bf16[1,64,128,128]{3,2,1,0:T(8,128)(2,1)} %get-tuple-element.19) | data formatting | bytes 4194304
  16.8 1.8 fusion.93
  20.5 4.1 %copy.159 = bf16[1,64,128,128]{2,3,1,0:T(8,128)(2,1)} copy(bf16[1,64,128,128]{3,2,1,0:T(8,128)(2,1)} %get-tuple-element.18) | data formatting | bytes 4194304
  25.0 1.8 fusion.94
  29.3 3.1 %copy.132 = f32[128,1,2880]{2,1,0:T(1,128)} copy(f32[128,1,2880]{0,2,1:T(8,128)S(1)} %convolution_bitcast_fusion) | data formatting | bytes 2949120 | tf_op jit(solution)/shard_map/rmk,kd->rmd/dot_general | solution.py:150
  32.9 3.1 %copy.128 = f32[128,1,2880]{2,1,0:T(1,128)} copy(f32[128,1,2880]{0,2,1:T(8,128)S(1)} %convolution_bitcast_fusion.1) | data formatting | bytes 2949120 | tf_op jit(solution)/shard_map/rmk,kd->rmd/dot_general | solution.py:150
  39.3 102.9 %all-reduce.5.cloned.1.call-done = (f32[128,1,2880]{2,1,0:T(1,128)}, f32[128,1,2880]{2,1,0:T(1,128)}) async-done(((f32[128,1,2880]{2,1,0:T(1,128)}, f32[128,1,2880]{2,1,0:T(1,128)}), (f32[128,1,2880]{2,1,0:T(1,128)}, f32[128,1,2880]{2,1,0:T(1,128)})) %all-reduce.5.cloned.1.call-update) | async-done | bytes 2949136
  146.3 4.1 %all-to-all-start.2 = ((bf16[1,16,4,2880]{3,2,0,1:T(4,128)(2,1)}), bf16[1,16,4,2880]{3,2,0,1:T(4,128)(2,1)S(1)}, u32[]{:S(2)}, u32[]{:S(2)}) async-start(bf16[1,16,4,2880]{3,2,0,1:T(4,128)(2,1)} %reshape.675), calls=%async_computation.2 | async-start | bytes 753664 | tf_op jit(solution)/shard_map/all_to_all | solution.py:72
  152.7 1.0 scatter_custom_fusion
  155.3 6.9 %all-to-all-done.2 = bf16[1,16,4,2880]{3,2,0,1:T(4,128)(2,1)S(1)} async-done(((bf16[1,16,4,2880]{3,2,0,1:T(4,128)(2,1)}), bf16[1,16,4,2880]{3,2,0,1:T(4,128)(2,1)S(1)}, u32[]{:S(2)}, u32[]{:S(2)}) %all-to-all-start.2) | async-done | bytes 368672 | tf_op jit(solution)/shard_map/all_to_all | solution.py:72
  162.2 3.7 %all-to-all-start = ((bf16[1,16,4,2880]{3,2,0,1:T(4,128)(2,1)}), bf16[1,16,4,2880]{3,2,0,1:T(4,128)(2,1)S(1)}, u32[]{:S(2)}, u32[]{:S(2)}) async-start(bf16[1,16,4,2880]{3,2,0,1:T(4,128)(2,1)} %reshape.668), calls=%async_computation | async-start | bytes 753664 | tf_op jit(solution)/shard_map/all_to_all | solution.py:72
  166.2 6.1 %fusion.98 = f32[64,4,360]{2,0,1:T(8,128)S(1)} fusion(bf16[64,2880,1]{1,0,2:T(8,128)(2,1)S(1)} %reshape.787, bf16[4,2880,360]{1,2,0:T(8,128)(2,1)} %param.22), kind=kOutput, calls=%fused_computation.184 | convolution fusion | flops 530841600 | bytes 9031680 | tf_op jit(solution)/shard_map/merd,eqdf->meqrf/dot_general | solution.py:85
  172.2 9.9 %fusion.2 = bf16[1,1,64,2880]{3,2,0,1:T(8,128)(2,1)S(1)} fusion(bf16[4,360,2880]{2,1,0:T(8,128)(2,1)} %param.24, f32[64,4,360]{2,0,1:T(8,128)S(1)} %fusion.98, bf16[64,2880,1]{1,0,2:T(8,128)(2,1)S(1)} %reshape.787, bf16[4,2880,360]{1,2,0:T(8,128)(2,1)} %param.23), kind=kOutput, calls=%fused_computation.12 | convolution fusion | flops 1062604800 | bytes 17694720 | tf_op jit(solution)/shard_map/meqrf,eqfd->merd/dot_general | solution.py:94
  183.3 3.0 %reduce.8 = bf16[64,2880]{1,0:T(8,128)(2,1)S(1)} reduce(bf16[64,1,1,2880]{3,2,1,0:T(2,128)(2,1)S(1)} %bitcast.159, bf16[]{:T(256)} %broadcast.520), dimensions={1,2}, to_apply=%bitcast.153.reduce_sub_computation | reduce | bytes 737282
  186.3 1.1 reshape.797
  187.4 5.8 %all-to-all-start.3 = ((bf16[16,2,5760]{2,1,0:T(2,128)(2,1)}), bf16[16,2,5760]{2,1,0:T(2,128)(2,1)S(1)}, u32[]{:S(2)}, u32[]{:S(2)}) async-start(bf16[16,2,5760]{2,1,0:T(2,128)(2,1)} %reshape.797), calls=%async_computation.3 | async-start | bytes 737280 | tf_op jit(solution)/shard_map/all_to_all | solution.py:106
  193.4 6.1 %fusion.96 = f32[64,4,360]{2,0,1:T(8,128)S(1)} fusion(bf16[64,2880,1]{1,0,2:T(8,128)(2,1)S(1)} %reshape.785, bf16[4,2880,360]{1,2,0:T(8,128)(2,1)} %param.22), kind=kOutput, calls=%fused_computation.182 | convolution fusion | flops 530841600 | bytes 9031680 | tf_op jit(solution)/shard_map/merd,eqdf->meqrf/dot_general | solution.py:85
  199.5 9.9 %fusion.3 = bf16[1,1,64,2880]{3,2,0,1:T(8,128)(2,1)S(1)} fusion(bf16[4,360,2880]{2,1,0:T(8,128)(2,1)} %param.24, f32[64,4,360]{2,0,1:T(8,128)S(1)} %fusion.96, bf16[64,2880,1]{1,0,2:T(8,128)(2,1)S(1)} %reshape.785, bf16[4,2880,360]{1,2,0:T(8,128)(2,1)} %param.23), kind=kOutput, calls=%fused_computation.13 | convolution fusion | flops 1062604800 | bytes 17694720 | tf_op jit(solution)/shard_map/meqrf,eqfd->merd/dot_general | solution.py:94
  210.0 3.0 %reduce.9 = bf16[64,2880]{1,0:T(8,128)(2,1)S(1)} reduce(bf16[64,1,1,2880]{3,2,1,0:T(2,128)(2,1)S(1)} %bitcast.160, bf16[]{:T(256)} %broadcast.520), dimensions={1,2}, to_apply=%bitcast.154.reduce_sub_computation | reduce | bytes 737282
  213.0 1.1 reshape.799
  214.1 6.0 %all-to-all-start.1 = ((bf16[16,2,5760]{2,1,0:T(2,128)(2,1)}), bf16[16,2,5760]{2,1,0:T(2,128)(2,1)}, u32[]{:S(2)}, u32[]{:S(2)}) async-start(bf16[16,2,5760]{2,1,0:T(2,128)(2,1)} %reshape.799), calls=%async_computation.1 | async-start | bytes 737280 | tf_op jit(solution)/shard_map/all_to_all | solution.py:106
  222.0 10.0 %all-to-all-done.1 = bf16[16,2,5760]{2,1,0:T(2,128)(2,1)} async-done(((bf16[16,2,5760]{2,1,0:T(2,128)(2,1)}), bf16[16,2,5760]{2,1,0:T(2,128)(2,1)}, u32[]{:S(2)}, u32[]{:S(2)}) %all-to-all-start.1) | async-done | bytes 368672 | tf_op jit(solution)/shard_map/all_to_all | solution.py:106
  232.0 2.8 %reshape.800 = bf16[64,1,1,2880]{3,2,1,0:T(2,128)(2,1)S(1)} reshape(bf16[16,2,5760]{2,1,0:T(2,128)(2,1)} %all-to-all-done.1) | data formatting | bytes 737280
  (138 shorter events, 21.9 us)
Async XLA Ops:
  7.2 21.5 %copy-start = (bf16[256,2880]{0,1:T(8,128)(2,1)S(1)}, bf16[256,2880]{0,1:T(8,128)(2,1)}, u32[]{:S(2)}) copy-start(bf16[256,2880]{0,1:T(8,128)(2,1)} %param.20) | copy-start | bytes 4423684
  7.2 135.0 %all-reduce.5.cloned.1.call-start = ((), (), s32[]{:S(2)}) async-start(), calls=%async_computation.4 | async-start | bytes 6029312
  12.1 4.1 %copy-start.4 = (bf16[2,64,512]{2,1,0:T(8,128)(2,1)S(1)}, bf16[2,64,512]{2,1,0:T(8,128)(2,1)}, u32[]{:S(2)}) copy-start(bf16[2,64,512]{2,1,0:T(8,128)(2,1)} %param.15) | copy-start | bytes 393220
  12.1 4.3 %copy-start.8 = (s32[2,128]{1,0:T(2,128)S(1)}, s32[2,128]{1,0:T(2,128)}, u32[]{:S(2)}) copy-start(s32[2,128]{1,0:T(2,128)} %param.18) | copy-start | bytes 3076
  12.1 4.4 %copy-start.7 = (bf16[2,64,128]{2,1,0:T(8,128)(2,1)S(1)}, bf16[2,64,128]{2,1,0:T(8,128)(2,1)}, u32[]{:S(2)}) copy-start(bf16[2,64,128]{2,1,0:T(8,128)(2,1)} %param.16) | copy-start | bytes 98308
  16.4 2.6 %copy-start.1 = (bf16[1,64,128,128]{2,3,1,0:T(8,128)(2,1)S(1)}, bf16[1,64,128,128]{2,3,1,0:T(8,128)(2,1)}, u32[]{:S(2)}) copy-start(bf16[1,64,128,128]{2,3,1,0:T(8,128)(2,1)} %copy.162) | copy-start | bytes 6291460
  20.0 8.7 %collective-permute-start.1 = (bf16[1,64,1,256]{3,1,2,0:T(8,128)(2,1)S(1)}, bf16[1,64,1,256]{3,1,2,0:T(8,128)(2,1)S(1)}, u32[]{:S(2)}, u32[]{:S(2)}) collective-permute-start(bf16[1,64,1,256]{3,1,2,0:T(8,128)(2,1)S(1)} %get-tuple-element.24), channel_id=1, source_target_pairs={{0,1},{1,0},{2,3},{3,2},{4,5},{5,4},{6,7},{7,6},{8,9},{9,8},{10,11... | collective-permute-start | bytes 98312 | tf_op jit(solution)/shard_map/ppermute | solution.py:25
  24.7 2.3 copy-start.2
  26.8 1.4 copy-start.6
  28.1 4.3 %collective-permute-start = (bf16[1,64,1,256]{3,1,2,0:T(8,128)(2,1)S(1)}, bf16[1,64,1,256]{3,1,2,0:T(8,128)(2,1)S(1)}, u32[]{:S(2)}, u32[]{:S(2)}) collective-permute-start(bf16[1,64,1,256]{3,1,2,0:T(8,128)(2,1)S(1)} %get-tuple-element.20), channel_id=1, source_target_pairs={{0,1},{1,0},{2,3},{3,2},{4,5},{5,4},{6,7},{7,6},{8,9},{9,8},{10,11... | collective-permute-start | bytes 98312 | tf_op jit(solution)/shard_map/ppermute | solution.py:25
  36.0 2.0 copy-start.9
  36.0 108.1 %copy-start.5 = (bf16[2,8,2880]{2,1,0:T(8,128)(2,1)S(1)}, bf16[2,8,2880]{2,1,0:T(8,128)(2,1)}, u32[]{:S(2)}) copy-start(bf16[2,8,2880]{2,1,0:T(8,128)(2,1)} %param.19) | copy-start | bytes 276484
  36.0 114.4 %copy-start.3 = (bf16[2880,16]{0,1:T(8,128)(2,1)S(1)}, bf16[2880,16]{0,1:T(8,128)(2,1)}, u32[]{:S(2)}) copy-start(bf16[2880,16]{0,1:T(8,128)(2,1)} %param.21) | copy-start | bytes 276484
  146.3 16.0 %all-to-all-start.2 = ((bf16[1,16,4,2880]{3,2,0,1:T(4,128)(2,1)}), bf16[1,16,4,2880]{3,2,0,1:T(4,128)(2,1)S(1)}, u32[]{:S(2)}, u32[]{:S(2)}) async-start(bf16[1,16,4,2880]{3,2,0,1:T(4,128)(2,1)} %reshape.675), calls=%async_computation.2 | async-start | bytes 753664 | tf_op jit(solution)/shard_map/all_to_all | solution.py:72
  162.2 25.2 %all-to-all-start = ((bf16[1,16,4,2880]{3,2,0,1:T(4,128)(2,1)}), bf16[1,16,4,2880]{3,2,0,1:T(4,128)(2,1)S(1)}, u32[]{:S(2)}, u32[]{:S(2)}) async-start(bf16[1,16,4,2880]{3,2,0,1:T(4,128)(2,1)} %reshape.668), calls=%async_computation | async-start | bytes 753664 | tf_op jit(solution)/shard_map/all_to_all | solution.py:72
  187.4 26.7 %all-to-all-start.3 = ((bf16[16,2,5760]{2,1,0:T(2,128)(2,1)}), bf16[16,2,5760]{2,1,0:T(2,128)(2,1)S(1)}, u32[]{:S(2)}, u32[]{:S(2)}) async-start(bf16[16,2,5760]{2,1,0:T(2,128)(2,1)} %reshape.797), calls=%async_computation.3 | async-start | bytes 737280 | tf_op jit(solution)/shard_map/all_to_all | solution.py:106
  214.1 17.8 %all-to-all-start.1 = ((bf16[16,2,5760]{2,1,0:T(2,128)(2,1)}), bf16[16,2,5760]{2,1,0:T(2,128)(2,1)}, u32[]{:S(2)}, u32[]{:S(2)}) async-start(bf16[16,2,5760]{2,1,0:T(2,128)(2,1)} %reshape.799), calls=%async_computation.1 | async-start | bytes 737280 | tf_op jit(solution)/shard_map/all_to_all | solution.py:106
Sparse Core Ops, SparseCore 0:
  36.1 106.0 all-reduce.4
where the time goes:
time: 244 us
  waiting for transfers between devices  120 us (49%)
  local copies, waits for them, and re-layouts  39.3 us (16%)
  matrix products  38.8 us (16%)
  starting transfers between devices  20.4 us (8%)
  between operations  15.3 us (6%)
  other arithmetic  9.88 us (4%)
    unnamed x2, waiting for transfers between devices  103 us
    dot_general x2, matrix products, expert_grouped(): jnp.einsum('meqrf,eqfd->merd', active, down_local, preferred_element_type...  19.8 us
    unnamed x30, local copies, waits for them, and re-layouts  16.8 us
    dot_general x2, matrix products, expert_grouped(): jnp.einsum('merd,eqdf->meqrf', arrived, gate_local, preferred_element_typ...  12.1 us
    all_to_all x2, starting transfers between devices, expert_grouped(): lax.all_to_all(partial_out.astype(jnp.bfloat16), 'req', split_axis=2, con...  11.8 us
    all_to_all x2, waiting for transfers between devices, expert_grouped(): lax.all_to_all(partial_out.astype(jnp.bfloat16), 'req', split_axis=2, con...  9.97 us
    all_to_all x2, starting transfers between devices, expert_grouped(): lax.all_to_all(sent, 'req', split_axis=1, concat_axis=2, tiled=True)  7.83 us
    all_to_all x2, waiting for transfers between devices, expert_grouped(): lax.all_to_all(sent, 'req', split_axis=1, concat_axis=2, tiled=True)  6.93 us
  transfers between devices with their start and end apart: 7, of which 3 were waited for; matrix products, arithmetic and copies ran while one was open for 26% of the time, Pallas kernels for 0%

commit v1 on v0

v1 whole, which is shorter than its diff:
```python
import functools
import math

import jax
import jax.numpy as jnp
from jax import lax
from jax.experimental import pallas as pl
from jax.experimental.pallas import tpu as pltpu
from jax.sharding import PartitionSpec as P

HD = 64
LANES = 128
EPS = 1e-05
MESH = pl.DeviceIdType.MESH


def flip(value, mask):
    bit = 1
    result = value
    while bit <= mask:
        if mask & bit:
            result = result + bit - 2 * bit * ((value // bit) % 2)
        bit *= 2
    return result


def exclusive(left, right, bits):
    result = left * 0
    for b in range(bits):
        x = (left // (1 << b)) % 2
        y = (right // (1 << b)) % 2
        result = result + (x + y - 2 * x * y) * (1 << b)
    return result


def layer_kernel(
    cfg,
    q_ref, nk_ref, bias_ref, cache_ref, res_ref, o_ref, router_ref, gate_ref, up_ref, down_ref, routes_ref,
    att_ref, lay_ref,
    cache_v, o_v, gate_v, up_v, down_v, mixed_v, heads_v, block_v, lhs_v,
    acc0, acc1, send0, send1, first0, first1, second0, second1, rows0, rows1, gates_v, wide_v, out0, out1,
    cache_sem, load_sem, swap_sem, rs_sem, ag_sem,
):
    n, levels, group, width, subs, splits, per_expert = cfg
    me = lax.axis_index("req")
    mine = me % group
    accs, sends = (acc0, acc1), (send0, send1)
    landings = ((first0, first1), (second0, second1))
    rows = (rows0, rows1)
    outs = (out0, out1)
    orders = [list(range(levels)), list(range(levels))]
    if levels > 2:
        orders[1][1], orders[1][2] = 2, 1
    starts = (0, splits[0])
    batches = cache_ref.shape[0]
    rank = levels

    def cache_copy(s, m):
        return pltpu.make_async_copy(
            cache_ref.at[m, pl.ds(s * 8, 8)], cache_v.at[s, m], cache_sem.at[s, m]
        )

    for s in range(subs):
        for m in range(batches):
            cache_copy(s, m).start()
    loads = [
        pltpu.make_async_copy(src, dst, load_sem.at[i])
        for i, (src, dst) in enumerate(
            ((o_ref, o_v), (gate_ref, gate_v), (up_ref, up_v), (down_ref, down_v))
        )
    ]
    for load in loads:
        load.start()

    masks = sorted({1 << d for d in range(levels)} | set(range(1, group)))
    barrier = pltpu.get_barrier_semaphore()
    for mask in masks:
        pl.semaphore_signal(barrier, inc=1, device_id={"req": flip(me, mask)}, device_id_type=MESH)

    factor = 1.0 / math.sqrt(HD)
    lane = lax.broadcasted_iota(jnp.int32, (16, LANES), 1)

    def attend(s, carry):
        for m in range(batches):
            cache_copy(s, m).wait()
        scores = []
        for r in range(16):
            keys = cache_v[s, r // 8, r % 8]
            scores.append(
                lax.dot_general(
                    q_ref[s * 16 + r], keys, (((1,), (1,)), ((), ())), preferred_element_type=jnp.float32
                )
            )
        scores = jnp.concatenate(scores, axis=0) * factor
        bias = jnp.broadcast_to(bias_ref[s][:, None, :], (16, 8, LANES)).reshape(128, LANES)
        fresh = jnp.broadcast_to(nk_ref[s].astype(jnp.float32)[:, None, :], (16, 8, LANES)).reshape(128, LANES)
        query = q_ref[pl.ds(s * 16, 16)].astype(jnp.float32).reshape(128, LANES)
        own = jnp.sum(query * fresh, axis=1, keepdims=True) * factor
        masked = scores + bias
        top = jnp.maximum(jnp.max(masked, axis=1, keepdims=True), own)
        weight = jnp.exp(masked - top)
        weight_own = jnp.exp(own - top)
        total = jnp.sum(weight, axis=1, keepdims=True) + weight_own
        probs = weight / total
        prob_own = (weight_own / total).astype(jnp.bfloat16).astype(jnp.float32)
        mixed = []
        for r in range(16):
            mixed.append(
                jnp.dot(
                    probs[r * 8 : r * 8 + 8].astype(jnp.bfloat16),
                    cache_v[s, r // 8, r % 8],
                    preferred_element_type=jnp.float32,
                )
            )
        mixed_v[...] = jnp.concatenate(mixed, axis=0) + prob_own * fresh
        head = [mixed_v[pl.ds(h, 16, stride=8), :] for h in range(8)]
        if width >= LANES:
            for j in range(4):
                pair = jnp.where(lane < HD, pltpu.roll(head[2 * j], HD, 1), head[2 * j + 1])
                dest, col = j * LANES // width, j * LANES % width
                heads_v[dest, s, :, col : col + LANES] = pair.astype(jnp.bfloat16)
        else:
            for h in range(8):
                heads_v[h, s] = pltpu.roll(head[h], HD, 1)[:, :HD].astype(jnp.bfloat16)
        return carry

    lax.fori_loop(0, subs, attend, 0)
    pl.semaphore_wait(barrier, len(masks))

    swaps = []
    for j in range(1, group):
        partner = flip(me, j)
        swap = pltpu.make_async_remote_copy(
            src_ref=heads_v.at[partner % group],
            dst_ref=block_v.at[j],
            send_sem=swap_sem.at[0, j],
            recv_sem=swap_sem.at[1, j],
            device_id={"req": partner},
            device_id_type=MESH,
        )
        swap.start()
        swaps.append(swap)
    block_v[0] = heads_v[mine]
    loads[0].wait()
    for swap in swaps:
        swap.wait()
    group_bits = group.bit_length() - 1
    for place in range(n):
        mask = sum(((place >> (levels - 1 - d)) & 1) << d for d in range(levels))
        dest = flip(me, mask)
        slot = exclusive(dest // subs % group, mine, group_bits)
        lhs_v[place] = block_v[slot, dest % subs]

    def region(order, level, bit):
        index = [slice(None)] * rank
        for d in order[:level]:
            index[d] = 0
        index[order[level]] = bit
        return tuple(index)

    def scatter_sum(phase):
        landing = landings[phase]
        copies = {}
        for level in range(levels):
            for c in range(2):
                order = orders[c]
                if level:
                    copies[level - 1, c].wait_recv()
                    done = region(order, level - 1, 1)
                    kept = region(order, level - 1, 0)
                    accs[c][kept] = accs[c][kept] + landing[c][done].astype(jnp.float32)
                out = region(order, level, 1)
                sends[c][out] = accs[c][out].astype(jnp.bfloat16)
                copies[level, c] = pltpu.make_async_remote_copy(
                    src_ref=sends[c].at[out],
                    dst_ref=landing[c].at[out],
                    send_sem=rs_sem.at[phase, 0, level, c],
                    recv_sem=rs_sem.at[phase, 1, level, c],
                    device_id={"req": flip(me, 1 << order[level])},
                    device_id_type=MESH,
                )
                copies[level, c].start()
        total = []
        for c in range(2):
            copies[levels - 1, c].wait_recv()
            last = region(orders[c], levels - 1, 1)
            kept = region(orders[c], levels - 1, 0)
            total.append(accs[c][kept] + landing[c][last].astype(jnp.float32))
        for copy in copies.values():
            copy.wait_send()
        return total

    lhs = lhs_v[...].reshape(n * 16, width)
    for c in range(2):
        part = jnp.dot(lhs, o_v[:, starts[c] : starts[c] + splits[c]], preferred_element_type=jnp.float32)
        accs[c][...] = part.reshape(accs[c].shape)
    summed = scatter_sum(0)

    own_place = (0,) * rank
    depth = splits[0] + splits[1]
    square = jnp.zeros((16, 1), jnp.float32)
    attended = []
    for c in range(2):
        cols = slice(starts[c], starts[c] + splits[c])
        held = jnp.concatenate([res_ref[m, :, cols].astype(jnp.float32) for m in range(2)], axis=0)
        value = (held + summed[c]).astype(jnp.bfloat16)
        for m in range(2):
            att_ref[m, :, cols] = value[m * 8 : m * 8 + 8]
        value = value.astype(jnp.float32)
        wide_v[:, cols] = value
        attended.append(value)
        square = square + jnp.sum(value * value, axis=1, keepdims=True)
    scale = lax.rsqrt(square / depth + EPS)
    logits = 0.0
    for c in range(2):
        normed = (attended[c] * scale).astype(jnp.bfloat16)
        rows[c][own_place] = normed
        logits = logits + jnp.dot(
            normed, router_ref[starts[c] : starts[c] + splits[c], :], preferred_element_type=jnp.float32
        )
    experts = router_ref.shape[1]
    ids = lax.broadcasted_iota(jnp.int32, (16, experts), 1)
    routes = routes_ref[...]
    named = jnp.zeros((16, experts), jnp.float32)
    for t in range(routes_ref.shape[1]):
        named = jnp.where(ids == routes[:, t : t + 1], 1.0, named)
    live = jnp.where(named > 0.0, logits, -jnp.inf)
    power = jnp.exp(live - jnp.max(live, axis=1, keepdims=True))
    gates = power / jnp.sum(power, axis=1, keepdims=True)
    gates_v[own_place] = jnp.concatenate([gates, jnp.zeros((16, LANES - experts), jnp.float32)], axis=1)

    streams = ((rows0, orders[0]), (rows1, orders[1]), (gates_v, orders[0]))
    copies = {}
    for level in reversed(range(levels)):
        for c, (ref, order) in enumerate(streams):
            if level < levels - 1:
                copies[level + 1, c].wait_recv()
            copies[level, c] = pltpu.make_async_remote_copy(
                src_ref=ref.at[region(order, level, 0)],
                dst_ref=ref.at[region(order, level, 1)],
                send_sem=ag_sem.at[0, level, c],
                recv_sem=ag_sem.at[1, level, c],
                device_id={"req": flip(me, 1 << order[level])},
                device_id_type=MESH,
            )
            copies[level, c].start()
    for c in range(3):
        copies[0, c].wait_recv()
    for copy in copies.values():
        copy.wait_send()
    for load in loads[1:]:
        load.wait()

    entries = gate_ref.shape[0]
    expert = me * entries // per_expert
    tiles = n // 16
    tile_bits = tiles.bit_length() - 1

    def tile_body(tile, carry):
        lead = tuple((tile // (1 << (tile_bits - 1 - b))) % 2 for b in range(tile_bits))
        at = lead + (slice(None),) * (rank - tile_bits)

        def entry_body(j, inner):
            hidden = []
            for weights in (gate_v, up_v):
                value = 0.0
                for c in range(2):
                    x = rows[c][at].reshape(256, splits[c])
                    value = value + jnp.dot(
                        x, weights[j, starts[c] : starts[c] + splits[c], :], preferred_element_type=jnp.float32
                    )
                hidden.append(value)
            g, u = hidden
            active = ((u + 1.0) * g * jax.nn.sigmoid(1.702 * g)).astype(jnp.bfloat16)
            for c in range(2):
                part = jnp.dot(
                    active, down_v[j, :, starts[c] : starts[c] + splits[c]], preferred_element_type=jnp.float32
                )
                outs[c][...] = jnp.where(j == 0, 0.0, outs[c][...]) + part
            return inner

        lax.fori_loop(0, entries, entry_body, 0)
        wide_gates = gates_v[at].reshape(256, LANES)
        column = lax.broadcasted_iota(jnp.int32, (256, LANES), 1)
        gate = jnp.sum(jnp.where(column == expert, wide_gates, 0.0), axis=1, keepdims=True)
        for c in range(2):
            part = jnp.where(gate > 0.0, outs[c][...] * gate, 0.0)
            accs[c][at] = part.reshape((2,) * (rank - tile_bits) + (16, splits[c]))
        return carry

    for c in range(2):
        outs[c][...] = jnp.zeros_like(outs[c])
    lax.fori_loop(0, tiles, tile_body, 0)
    mixture = scatter_sum(1)
    for c in range(2):
        cols = slice(starts[c], starts[c] + splits[c])
        value = (wide_v[:, cols] + mixture[c]).astype(jnp.bfloat16)
        for m in range(2):
            lay_ref[m, :, cols] = value[m * 8 : m * 8 + 8]


def shards(queries, new_kv, cache, lengths, residual, o_proj, router, w_gate, w_up, w_down, routes):
    n = lax.axis_size("req")
    me = lax.axis_index("req")
    levels = n.bit_length() - 1
    batches, local, q_cols = queries.shape
    depth = residual.shape[2]
    own_rows = residual.shape[1]
    window = cache.shape[2]
    width = o_proj.shape[0]
    group = q_cols // width
    subs = local // own_rows
    heads = q_cols // HD
    per_expert = max(1, n * w_gate.shape[0] // router.shape[1])
    cut = (depth // 2 + LANES - 1) // LANES * LANES
    splits = (cut, depth - cut)

    def by_place(x):
        x = x.reshape((batches, subs, own_rows) + x.shape[2:])
        x = jnp.swapaxes(x, 0, 1)
        return x.reshape((subs, batches * own_rows) + x.shape[3:])

    live = lax.dynamic_slice_in_dim(lengths, me % group * local, local, 1)
    bias = jnp.where(jnp.arange(window)[None, None, :] < live[:, :, None], 0.0, -jnp.inf).astype(jnp.float32)
    query = jnp.pad(queries.reshape(batches, local, heads, HD), ((0, 0), (0, 0), (0, 0), (0, HD)))
    query = by_place(query).reshape(batches * local, heads, 2 * HD)

    cube = (2,) * levels
    f32, b16 = jnp.float32, jnp.bfloat16
    rows = batches * own_rows
    vmem = pl.BlockSpec(memory_space=pltpu.VMEM)
    hbm = pl.BlockSpec(memory_space=pl.ANY)

    def pair(dtype):
        return [pltpu.VMEM(cube + (rows, s), dtype) for s in splits]

    scratch = [
        pltpu.VMEM((subs, batches, own_rows) + cache.shape[2:], b16),
        pltpu.VMEM(o_proj.shape, b16),
        pltpu.VMEM(w_gate.shape, b16),
        pltpu.VMEM(w_up.shape, b16),
        pltpu.VMEM(w_down.shape, b16),
        pltpu.VMEM((rows * heads, LANES), f32),
        pltpu.VMEM((group, subs, rows, width), b16),
        pltpu.VMEM((group, subs, rows, width), b16),
        pltpu.VMEM((n, rows, width), b16),
        *pair(f32), *pair(b16), *pair(b16), *pair(b16), *pair(b16),
        pltpu.VMEM(cube + (rows, LANES), f32),
        pltpu.VMEM((rows, depth), f32),
        *[pltpu.VMEM((256, s), f32) for s in splits],
        pltpu.SemaphoreType.DMA((subs, batches)),
        pltpu.SemaphoreType.DMA((4,)),
        pltpu.SemaphoreType.DMA((2, group)),
        pltpu.SemaphoreType.DMA((2, 2, levels, 2)),
        pltpu.SemaphoreType.DMA((2, levels, 3)),
    ]
    out = jax.ShapeDtypeStruct(residual.shape, b16)
    return pl.pallas_call(
        functools.partial(layer_kernel, (n, levels, group, width, subs, splits, per_expert)),
        out_shape=(out, out),
        in_specs=[vmem, vmem, vmem, hbm, vmem, hbm, vmem, hbm, hbm, hbm, vmem],
        out_specs=(vmem, vmem),
        scratch_shapes=scratch,
        compiler_params=pltpu.CompilerParams(
            collective_id=0, has_side_effects=True, vmem_limit_bytes=67043328
        ),
        name="moe_layer",
    )(
        query, by_place(new_kv), by_place(bias), cache, residual, o_proj, router, w_gate, w_up, w_down,
        routes.reshape(rows, routes.shape[2]),
    )


def solution(mesh):
    placed = (
        P(None, ("groups", "req"), None),
        P(None, ("groups", "req"), None),
        P(None, ("groups", "req"), None, None),
        P(None, "groups"),
        P(None, ("groups", "req"), None),
        P("req", None),
        P(),
        P("req", None, None),
        P("req", None, None),
        P("req", None, None),
        P(None, ("groups", "req"), None),
    )
    if tuple(mesh.axis_names) != ("groups", "req"):
        raise ValueError("mesh axes")
    return jax.shard_map(
        shards,
        mesh=mesh,
        in_specs=placed,
        out_specs=(P(None, ("groups", "req"), None), P(None, ("groups", "req"), None)),
        check_vma=False,
    )
```

time: 244 us -> 117 us (0.48)
  waiting for transfers between devices: 120 us -> 0 us
  Pallas kernels: 0 us -> 78.5 us
  matrix products: 38.8 us -> 0 us
  starting transfers between devices: 20.4 us -> 0 us
  between operations: 15.3 us -> 0.67 us
  other arithmetic: 9.88 us -> 0.71 us
  local copies, waits for them, and re-layouts: 39.3 us -> 36.5 us
    unnamed x2 -> x0, waiting for transfers between devices: 103 us -> none
    pallas_call x0 -> x1, Pallas kernels: none -> 78.5 us  [shards(): pl.pallas_call(functools.partial(layer_kernel, (n, levels, group, width,...]
    dot_general x14 -> x0, matrix products: 38.8 us -> none  [the longest x2 19.8 us: expert_grouped(): jnp.einsum('meqrf,eqfd->merd', active, down_local, preferred_element_type...]
    all_to_all x4 -> x0, starting transfers between devices: 19.7 us -> none  [the longest x2 11.8 us: expert_grouped(): lax.all_to_all(partial_out.astype(jnp.bfloat16), 'req', split_axis=2, con...]
    all_to_all x4 -> x0, waiting for transfers between devices: 16.9 us -> none  [the longest x2 9.97 us: expert_grouped(): lax.all_to_all(partial_out.astype(jnp.bfloat16), 'req', split_axis=2, con...]
    unnamed x30 -> x6, local copies, waits for them, and re-layouts: 16.8 us -> 31 us
    dot_general x2 -> x0, local copies, waits for them, and re-layouts: 6.17 us -> none  [process_batches(): jnp.einsum('rmk,kd->rmd', head_rows, o_proj, preferred_element_type=jnp.f...]
    unnamed x2 -> x0, other arithmetic: 5.97 us -> none
  transfers between devices with their start and end apart: 7 -> 0, of which waited for: 3 -> 0; matrix products, arithmetic and copies ran while one was open for 26% -> 0% of each run, Pallas kernels for 0% -> 0%
where the time goes in v1:
time: 117 us; the launch traced here: 116 us
  Pallas kernels  78.5 us (67%)
  local copies, waits for them, and re-layouts  36.5 us (31%)
    pallas_call x1, Pallas kernels, shards(): pl.pallas_call(functools.partial(layer_kernel, (n, levels, group, width,...  78.5 us
    unnamed x6, local copies, waits for them, and re-layouts  31 us

profile of v1, /device:TPU:0, one launch (start us, length us, event | category | flops | bytes accessed | tf_op | source)
XLA Modules:
  0.0 116.3 jit_solution(4157185884717564892)
XLA Ops:
  0.6 0.8 constant_dynamic-slice_fusion
  1.4 0.1 lt.34
  1.5 0.1 lt.36
  1.6 1.4 %copy.30 = s32[2,8,4]{2,1,0:T(8,128)} copy(s32[2,8,4]{1,2,0:T(4,128)} %param.21) | data formatting | bytes 512 | tf_op jit(solution)/shard_map/reshape | solution.py:370
  2.9 1.4 %copy_bitcast_fusion.nk_ref = bf16[8,16,128]{2,1,0:T(8,128)(2,1)} fusion(bf16[2,64,128]{2,1,0:T(8,128)(2,1)} %param.12), kind=kLoop, calls=%fused_computation.2 | loop fusion | bytes 65536 | tf_op jit(solution)/shard_map/reshape | solution.py:321
  4.3 0.7 fusion.bias_ref
  5.0 1.1 reshape.26
  6.1 0.1 pad.4
  6.2 0.7 copy.21
  6.9 2.0 %copy.26.router_ref = bf16[2880,16]{1,0:T(8,128)(2,1)} copy(bf16[2880,16]{0,1:T(8,128)(2,1)} %param.17) | data formatting | bytes 184320 | tf_op args[6]
  9.0 2.6 %copy.25.o_ref = bf16[256,2880]{1,0:T(8,128)(2,1)} copy(bf16[256,2880]{0,1:T(8,128)(2,1)} %param.16) | data formatting | bytes 2949120 | tf_op args[5]
  11.5 11.6 %copy.27.gate_ref = bf16[4,2880,360]{2,1,0:T(8,128)(2,1)} copy(bf16[4,2880,360]{1,2,0:T(8,128)(2,1)} %param.18) | data formatting | bytes 16588800 | tf_op args[7]
  23.2 11.6 %copy.28.up_ref = bf16[4,2880,360]{2,1,0:T(8,128)(2,1)} copy(bf16[4,2880,360]{1,2,0:T(8,128)(2,1)} %param.19) | data formatting | bytes 16588800 | tf_op args[8]
  34.8 78.5 %moe_layer.1 = (bf16[2,8,2880]{2,1,0:T(8,128)(2,1)}, bf16[2,8,2880]{2,1,0:T(8,128)(2,1)}) custom-call(bf16[128,8,128]{2,1,0:T(8,128)(2,1)} %bitcast.13, bf16[8,16,128]{2,1,0:T(8,128)(2,1)} %copy_bitcast_fusion.nk_ref, f32[8,16,128]{2,1,0:T(8,128)} %fusion.bias_ref, bf16[2,64,128,128]{3,2,1,0:T(8,128)(2,1)} %cache_ref.1, bf16[2,8,2880]{2,1,0:T(8,128)(2,1)} %res_ref.1, ...), custom_call_target="tpu_custom_call" | custom-call | tf_op jit(solution)/shard_map/moe_layer/pallas_call | solution.py:358
  113.3 1.5 %copy.35 = bf16[2,8,2880]{2,1,0:T(8,128)(2,1)} copy(bf16[2,8,2880]{2,1,0:T(8,128)(2,1)} %get-tuple-element.4) | data formatting | bytes 184320
  114.8 1.5 %copy.36 = bf16[2,8,2880]{2,1,0:T(8,128)(2,1)} copy(bf16[2,8,2880]{2,1,0:T(8,128)(2,1)} %get-tuple-element.5) | data formatting | bytes 184320
  (1 shorter events, 0.0 us)

commit v2 on v1

--- a/solution.py
+++ b/solution.py
@@ -33,11 +33,15 @@
     return result
 
 
+def dot_t(left, right):
+    return lax.dot_general(left, right, (((1,), (1,)), ((), ())), preferred_element_type=jnp.float32)
+
+
 def layer_kernel(
     cfg,
-    q_ref, nk_ref, bias_ref, cache_ref, res_ref, o_ref, router_ref, gate_ref, up_ref, down_ref, routes_ref,
+    q_ref, nk_ref, len_ref, cache_ref, res_ref, o_ref, router_ref, gate_ref, up_ref, down_ref, routes_ref,
     att_ref, lay_ref,
-    cache_v, o_v, gate_v, up_v, down_v, mixed_v, heads_v, block_v, lhs_v,
+    cache_v, o_v, gate_v, up_v, down_v, query_v, mixed_v, heads_v, block_v, lhs_v,
     acc0, acc1, send0, send1, first0, first1, second0, second1, rows0, rows1, gates_v, wide_v, out0, out1,
     cache_sem, load_sem, swap_sem, rs_sem, ag_sem,
 ):
@@ -79,24 +83,28 @@
 
     factor = 1.0 / math.sqrt(HD)
     lane = lax.broadcasted_iota(jnp.int32, (16, LANES), 1)
+    position = lax.broadcasted_iota(jnp.int32, (8, LANES), 1)
+    first = mine * subs * 8
 
     def attend(s, carry):
         for m in range(batches):
             cache_copy(s, m).wait()
-        scores = []
+        here = pl.ds(pl.multiple_of(s * 8, 8), 8)
+        fresh = jnp.concatenate([nk_ref[m, here, :].astype(jnp.float32) for m in range(batches)], axis=0)
+        fresh = jnp.broadcast_to(fresh[:, None, :], (16, 8, LANES)).reshape(128, LANES)
+        for j in range(4):
+            pair = jnp.concatenate(
+                [q_ref[m, here, j * LANES : (j + 1) * LANES].astype(jnp.float32) for m in range(batches)], axis=0
+            )
+            query_v[pl.ds(2 * j, 16, stride=8), :] = jnp.where(lane < HD, pair, 0.0)
+            query_v[pl.ds(2 * j + 1, 16, stride=8), :] = jnp.where(lane < HD, pltpu.roll(pair, HD, 1), 0.0)
+        masked = []
         for r in range(16):
-            keys = cache_v[s, r // 8, r % 8]
-            scores.append(
-                lax.dot_general(
-                    q_ref[s * 16 + r], keys, (((1,), (1,)), ((), ())), preferred_element_type=jnp.float32
-                )
-            )
-        scores = jnp.concatenate(scores, axis=0) * factor
-        bias = jnp.broadcast_to(bias_ref[s][:, None, :], (16, 8, LANES)).reshape(128, LANES)
-        fresh = jnp.broadcast_to(nk_ref[s].astype(jnp.float32)[:, None, :], (16, 8, LANES)).reshape(128, LANES)
-        query = q_ref[pl.ds(s * 16, 16)].astype(jnp.float32).reshape(128, LANES)
-        own = jnp.sum(query * fresh, axis=1, keepdims=True) * factor
-        masked = scores + bias
+            score = dot_t(query_v[r * 8 : r * 8 + 8, :].astype(jnp.bfloat16), cache_v[s, r // 8, r % 8])
+            live = position < len_ref[r // 8, first + s * 8 + r % 8]
+            masked.append(jnp.where(live, score * factor, -jnp.inf))
+        masked = jnp.concatenate(masked, axis=0)
+        own = jnp.sum(query_v[...] * fresh, axis=1, keepdims=True) * factor
         top = jnp.maximum(jnp.max(masked, axis=1, keepdims=True), own)
         weight = jnp.exp(masked - top)
         weight_own = jnp.exp(own - top)
@@ -192,7 +200,7 @@
 
     lhs = lhs_v[...].reshape(n * 16, width)
     for c in range(2):
-        part = jnp.dot(lhs, o_v[:, starts[c] : starts[c] + splits[c]], preferred_element_type=jnp.float32)
+        part = dot_t(lhs, o_v[starts[c] : starts[c] + splits[c], :])
         accs[c][...] = part.reshape(accs[c].shape)
     summed = scatter_sum(0)
 
@@ -215,12 +223,15 @@
     for c in range(2):
         normed = (attended[c] * scale).astype(jnp.bfloat16)
         rows[c][own_place] = normed
-        logits = logits + jnp.dot(
-            normed, router_ref[starts[c] : starts[c] + splits[c], :], preferred_element_type=jnp.float32
-        )
-    experts = router_ref.shape[1]
-    ids = lax.broadcasted_iota(jnp.int32, (16, experts), 1)
-    routes = routes_ref[...]
+        logits = logits + dot_t(normed, router_ref[:, starts[c] : starts[c] + splits[c]])
+    experts = router_ref.shape[0]
+    ids = lax.broadcasted_iota(jnp.int32, (16, experts), 1).astype(jnp.float32)
+    row = lax.broadcasted_iota(jnp.int32, (16, 8), 0)
+    col = lax.broadcasted_iota(jnp.int32, (16, 8), 1)
+    routes = 0.0
+    for m in range(batches):
+        pick = jnp.where(row == col + m * 8, 1.0, 0.0).astype(jnp.bfloat16)
+        routes = routes + dot_t(pick, routes_ref[m].astype(jnp.float32).astype(jnp.bfloat16))
     named = jnp.zeros((16, experts), jnp.float32)
     for t in range(routes_ref.shape[1]):
         named = jnp.where(ids == routes[:, t : t + 1], 1.0, named)
@@ -266,9 +277,7 @@
                 value = 0.0
                 for c in range(2):
                     x = rows[c][at].reshape(256, splits[c])
-                    value = value + jnp.dot(
-                        x, weights[j, starts[c] : starts[c] + splits[c], :], preferred_element_type=jnp.float32
-                    )
+                    value = value + dot_t(x, weights[j, :, starts[c] : starts[c] + splits[c]])
                 hidden.append(value)
             g, u = hidden
             active = ((u + 1.0) * g * jax.nn.sigmoid(1.702 * g)).astype(jnp.bfloat16)
@@ -301,12 +310,10 @@
 
 def shards(queries, new_kv, cache, lengths, residual, o_proj, router, w_gate, w_up, w_down, routes):
     n = lax.axis_size("req")
-    me = lax.axis_index("req")
     levels = n.bit_length() - 1
     batches, local, q_cols = queries.shape
     depth = residual.shape[2]
     own_rows = residual.shape[1]
-    window = cache.shape[2]
     width = o_proj.shape[0]
     group = q_cols // width
     subs = local // own_rows
@@ -315,20 +322,12 @@
     cut = (depth // 2 + LANES - 1) // LANES * LANES
     splits = (cut, depth - cut)
 
-    def by_place(x):
-        x = x.reshape((batches, subs, own_rows) + x.shape[2:])
-        x = jnp.swapaxes(x, 0, 1)
-        return x.reshape((subs, batches * own_rows) + x.shape[3:])
-
-    live = lax.dynamic_slice_in_dim(lengths, me % group * local, local, 1)
-    bias = jnp.where(jnp.arange(window)[None, None, :] < live[:, :, None], 0.0, -jnp.inf).astype(jnp.float32)
-    query = jnp.pad(queries.reshape(batches, local, heads, HD), ((0, 0), (0, 0), (0, 0), (0, HD)))
-    query = by_place(query).reshape(batches * local, heads, 2 * HD)
-
+    gate_t, up_t = jnp.swapaxes(w_gate, 1, 2), jnp.swapaxes(w_up, 1, 2)
     cube = (2,) * levels
     f32, b16 = jnp.float32, jnp.bfloat16
     rows = batches * own_rows
     vmem = pl.BlockSpec(memory_space=pltpu.VMEM)
+    smem = pl.BlockSpec(memory_space=pltpu.SMEM)
     hbm = pl.BlockSpec(memory_space=pl.ANY)
 
     def pair(dtype):
@@ -336,10 +335,11 @@
 
     scratch = [
         pltpu.VMEM((subs, batches, own_rows) + cache.shape[2:], b16),
-        pltpu.VMEM(o_proj.shape, b16),
-        pltpu.VMEM(w_gate.shape, b16),
-        pltpu.VMEM(w_up.shape, b16),
+        pltpu.VMEM(o_proj.shape[::-1], b16),
+        pltpu.VMEM(gate_t.shape, b16),
+        pltpu.VMEM(up_t.shape, b16),
         pltpu.VMEM(w_down.shape, b16),
+        pltpu.VMEM((rows * heads, LANES), f32),
         pltpu.VMEM((rows * heads, LANES), f32),
         pltpu.VMEM((group, subs, rows, width), b16),
         pltpu.VMEM((group, subs, rows, width), b16),
@@ -358,7 +358,7 @@
     return pl.pallas_call(
         functools.partial(layer_kernel, (n, levels, group, width, subs, splits, per_expert)),
         out_shape=(out, out),
-        in_specs=[vmem, vmem, vmem, hbm, vmem, hbm, vmem, hbm, hbm, hbm, vmem],
+        in_specs=[vmem, vmem, smem, hbm, vmem, hbm, vmem, hbm, hbm, hbm, vmem],
         out_specs=(vmem, vmem),
         scratch_shapes=scratch,
         compiler_params=pltpu.CompilerParams(
@@ -366,8 +366,8 @@
         ),
         name="moe_layer",
     )(
-        query, by_place(new_kv), by_place(bias), cache, residual, o_proj, router, w_gate, w_up, w_down,
-        routes.reshape(rows, routes.shape[2]),
+        queries, new_kv, lengths, cache, residual, o_proj.T, router.T, gate_t, up_t, w_down,
+        jnp.swapaxes(routes, 1, 2),
     )
 
 

time: 117 us -> 82.3 us (0.70)
  local copies, waits for them, and re-layouts: 36.5 us -> 3.07 us
    unnamed x6 -> x2, local copies, waits for them, and re-layouts: 31 us -> 3.07 us
    reshape x3 -> x0, local copies, waits for them, and re-layouts: 3.84 us -> none  [the longest x1 1.38 us: by_place(): return x.reshape((subs, batches * own_rows) + x.shape[3:])]
where the time goes in v2:
time: 82.3 us; the launch traced here: 82.1 us
  Pallas kernels  78.4 us (95%)
  local copies, waits for them, and re-layouts  3.07 us (4%)
    pallas_call x1, Pallas kernels, shards(): pl.pallas_call(functools.partial(layer_kernel, (n, levels, group, width,...  78.4 us
    unnamed x2, local copies, waits for them, and re-layouts  3.07 us

profile of v2, /device:TPU:0, one launch (start us, length us, event | category | flops | bytes accessed | tf_op | source)
XLA Modules:
  0.0 82.1 jit_solution(8859765531795100934)
XLA Ops:
  0.6 78.4 %moe_layer.1 = (bf16[2,8,2880]{2,1,0:T(8,128)(2,1)}, bf16[2,8,2880]{2,1,0:T(8,128)(2,1)}) custom-call(bf16[2,64,512]{2,1,0:T(8,128)(2,1)} %q_ref.1, bf16[2,64,128]{2,1,0:T(8,128)(2,1)} %nk_ref.1, s32[2,128]{1,0:T(2,128)} %len_ref.1, bf16[2,64,128,128]{3,2,1,0:T(8,128)(2,1)} %cache_ref.1, bf16[2,8,2880]{2,1,0:T(8,128)(2,1)} %res_ref.1, ...), custom_call_target="tpu_custom_call" | custom-call | tf_op jit(solution)/shard_map/moe_layer/pallas_call | solution.py:358
  79.0 1.5 %copy.15 = bf16[2,8,2880]{2,1,0:T(8,128)(2,1)} copy(bf16[2,8,2880]{2,1,0:T(8,128)(2,1)} %get-tuple-element.4) | data formatting | bytes 184320
  80.5 1.5 %copy.16 = bf16[2,8,2880]{2,1,0:T(8,128)(2,1)} copy(bf16[2,8,2880]{2,1,0:T(8,128)(2,1)} %get-tuple-element.5) | data formatting | bytes 184320

commit v3 on v2

v3 whole, which is shorter than its diff:
```python
import functools
import math

import jax
import jax.numpy as jnp
from jax import lax
from jax.experimental import pallas as pl
from jax.experimental.pallas import tpu as pltpu
from jax.sharding import PartitionSpec as P

HD = 64
LANES = 128
EPS = 1e-05
MESH = pl.DeviceIdType.MESH


def flip(value, mask):
    bit = 1
    result = value
    while bit <= mask:
        if mask & bit:
            result = result + bit - 2 * bit * ((value // bit) % 2)
        bit *= 2
    return result


def exclusive(left, right, bits):
    result = left * 0
    for b in range(bits):
        x = (left // (1 << b)) % 2
        y = (right // (1 << b)) % 2
        result = result + (x + y - 2 * x * y) * (1 << b)
    return result


def dot_t(left, right):
    return lax.dot_general(left, right, (((1,), (1,)), ((), ())), preferred_element_type=jnp.float32)


def layer_kernel(
    cfg,
    q_ref, nk_ref, len_ref, cache_ref, res_ref, o_ref, router_ref, gate_ref, up_ref, down_ref, routes_ref,
    att_ref, lay_ref,
    cache_v, o_v, gate_v, up_v, down_v, query_v, mixed_v, heads_v, block_v, lhs_v, wide_v,
    *more,
):
    n, levels, group, width, subs, splits, per_expert, batches = cfg
    more = list(more)

    def take(count):
        return [more.pop(0) for _ in range(count)]

    accs = [take(2) for _ in range(batches)]
    sends = [take(2) for _ in range(batches)]
    landings = [[take(2) for _ in range(2)] for _ in range(batches)]
    rows = [take(2) for _ in range(batches)]
    gates_v = take(batches)
    xs = [take(2) for _ in range(batches)]
    outs = [take(2) for _ in range(batches)]
    cache_sem, load_sem, swap_sem, rs_sem, ag_sem = more
    me = lax.axis_index("req")
    mine = me % group
    orders = [list(range(levels)), list(range(levels))]
    if levels > 2:
        orders[1][1], orders[1][2] = 2, 1
    starts = (0, splits[0])
    rank = levels
    own_place = (0,) * rank
    turns = subs // 2

    def cache_copy(m, k):
        return pltpu.make_async_copy(
            cache_ref.at[m, pl.ds(k * 16, 16)], cache_v.at[m, pl.ds(k * 16, 16)], cache_sem.at[m, k]
        )

    loads = [
        pltpu.make_async_copy(src, dst, load_sem.at[i])
        for i, (src, dst) in enumerate(
            ((o_ref, o_v), (gate_ref, gate_v), (up_ref, up_v), (down_ref, down_v))
        )
    ]
    for m in range(batches):
        for k in range(turns):
            cache_copy(m, k).start()
        if m == 0:
            loads[0].start()

    masks = sorted({1 << d for d in range(levels)} | set(range(1, group)))
    barrier = pltpu.get_barrier_semaphore()
    for mask in masks:
        pl.semaphore_signal(barrier, inc=1, device_id={"req": flip(me, mask)}, device_id_type=MESH)

    factor = 1.0 / math.sqrt(HD)
    lane = lax.broadcasted_iota(jnp.int32, (16, LANES), 1)
    position = lax.broadcasted_iota(jnp.int32, (8, LANES), 1)
    first = mine * subs * 8

    def attend(m, k):
        cache_copy(m, k).wait()
        base = k * 16
        here = pl.ds(pl.multiple_of(base, 16), 16)
        fresh = nk_ref[m, here, :].astype(jnp.float32)
        fresh = jnp.broadcast_to(fresh[:, None, :], (16, 8, LANES)).reshape(128, LANES)
        for j in range(4):
            pair = q_ref[m, here, j * LANES : (j + 1) * LANES].astype(jnp.float32)
            query_v[pl.ds(2 * j, 16, stride=8), :] = jnp.where(lane < HD, pair, 0.0)
            query_v[pl.ds(2 * j + 1, 16, stride=8), :] = jnp.where(lane < HD, pltpu.roll(pair, HD, 1), 0.0)
        masked = []
        for r in range(16):
            score = dot_t(query_v[r * 8 : r * 8 + 8, :].astype(jnp.bfloat16), cache_v[m, base + r])
            live = position < len_ref[m, first + base + r]
            masked.append(jnp.where(live, score * factor, -jnp.inf))
        masked = jnp.concatenate(masked, axis=0)
        own = jnp.sum(query_v[...] * fresh, axis=1, keepdims=True) * factor
        top = jnp.maximum(jnp.max(masked, axis=1, keepdims=True), own)
        weight = jnp.exp(masked - top)
        weight_own = jnp.exp(own - top)
        total = jnp.sum(weight, axis=1, keepdims=True) + weight_own
        probs = weight / total
        prob_own = (weight_own / total).astype(jnp.bfloat16).astype(jnp.float32)
        mixed = []
        for r in range(16):
            mixed.append(
                jnp.dot(
                    probs[r * 8 : r * 8 + 8].astype(jnp.bfloat16),
                    cache_v[m, base + r],
                    preferred_element_type=jnp.float32,
                )
            )
        mixed_v[...] = jnp.concatenate(mixed, axis=0) + prob_own * fresh
        head = [mixed_v[pl.ds(h, 16, stride=8), :] for h in range(8)]
        if width >= LANES:
            for j in range(4):
                pair = jnp.where(lane < HD, pltpu.roll(head[2 * j], HD, 1), head[2 * j + 1])
                dest, col = j * LANES // width, j * LANES % width
                for b in range(2):
                    heads_v[dest, m, 2 * k + b, :, col : col + LANES] = pair[b * 8 : b * 8 + 8]
        else:
            for h in range(8):
                one = pltpu.roll(head[h], HD, 1)[:, :HD]
                for b in range(2):
                    heads_v[h, m, 2 * k + b] = one[b * 8 : b * 8 + 8]

    def attend_range(m, low, high):
        def body(k, carry):
            attend(m, k)
            return carry

        lax.fori_loop(low, high, body, 0)

    def region(order, level, bit):
        index = [slice(None)] * rank
        for d in order[:level]:
            index[d] = 0
        index[order[level]] = bit
        return tuple(index)

    def scatter_step(m, phase, level, copies):
        for c in range(2):
            order, acc, landing = orders[c], accs[m][c], landings[m][phase][c]
            if level:
                copies[level - 1, c].wait_recv()
                done = region(order, level - 1, 1)
                kept = region(order, level - 1, 0)
                acc[kept] = acc[kept] + landing[done].astype(jnp.float32)
            out = region(order, level, 1)
            sends[m][c][out] = acc[out].astype(jnp.bfloat16)
            copies[level, c] = pltpu.make_async_remote_copy(
                src_ref=sends[m][c].at[out],
                dst_ref=landing.at[out],
                send_sem=rs_sem.at[m, phase, 0, level, c],
                recv_sem=rs_sem.at[m, phase, 1, level, c],
                device_id={"req": flip(me, 1 << order[level])},
                device_id_type=MESH,
            )
            copies[level, c].start()

    def scatter_end(m, phase, copies):
        total = []
        for c in range(2):
            copies[levels - 1, c].wait_recv()
            last = region(orders[c], levels - 1, 1)
            kept = region(orders[c], levels - 1, 0)
            total.append(accs[m][c][kept] + landings[m][phase][c][last].astype(jnp.float32))
        for copy in copies.values():
            copy.wait_send()
        return total

    def norm_rows(m, summed):
        square = jnp.zeros((8, 1), jnp.float32)
        attended = []
        for c in range(2):
            cols = slice(starts[c], starts[c] + splits[c])
            value = (res_ref[m, :, cols].astype(jnp.float32) + summed[c]).astype(jnp.bfloat16)
            att_ref[m, :, cols] = value
            value = value.astype(jnp.float32)
            wide_v[m, :, cols] = value
            attended.append(value)
            square = square + jnp.sum(value * value, axis=1, keepdims=True)
        scale = lax.rsqrt(square / (splits[0] + splits[1]) + EPS)
        logits = 0.0
        for c in range(2):
            normed = (attended[c] * scale).astype(jnp.bfloat16)
            rows[m][c][own_place] = normed
            logits = logits + dot_t(normed, router_ref[:, starts[c] : starts[c] + splits[c]])
        experts = router_ref.shape[0]
        ids = lax.broadcasted_iota(jnp.int32, (8, experts), 1).astype(jnp.float32)
        row = lax.broadcasted_iota(jnp.int32, (8, 8), 0)
        col = lax.broadcasted_iota(jnp.int32, (8, 8), 1)
        pick = jnp.where(row == col, 1.0, 0.0).astype(jnp.bfloat16)
        routes = dot_t(pick, routes_ref[m].astype(jnp.float32).astype(jnp.bfloat16))
        named = jnp.zeros((8, experts), jnp.float32)
        for t in range(routes_ref.shape[1]):
            named = jnp.where(ids == routes[:, t : t + 1], 1.0, named)
        live = jnp.where(named > 0.0, logits, -jnp.inf)
        power = jnp.exp(live - jnp.max(live, axis=1, keepdims=True))
        gates = power / jnp.sum(power, axis=1, keepdims=True)
        gates_v[m][own_place] = jnp.concatenate([gates, jnp.zeros((8, LANES - experts), jnp.float32)], axis=1)

    def gather_step(m, level, copies):
        streams = ((rows[m][0], orders[0]), (rows[m][1], orders[1]), (gates_v[m], orders[0]))
        for c, (ref, order) in enumerate(streams):
            if level < levels - 1:
                copies[level + 1, c].wait_recv()
            copies[level, c] = pltpu.make_async_remote_copy(
                src_ref=ref.at[region(order, level, 0)],
                dst_ref=ref.at[region(order, level, 1)],
                send_sem=ag_sem.at[m, 0, level, c],
                recv_sem=ag_sem.at[m, 1, level, c],
                device_id={"req": flip(me, 1 << order[level])},
                device_id_type=MESH,
            )
            copies[level, c].start()

    entries = gate_ref.shape[0]
    expert = me * entries // per_expert
    tiles = n // 16
    tile_bits = tiles.bit_length() - 1

    def expert_entry(m, tile, j):
        lead = tuple((tile >> (tile_bits - 1 - b)) & 1 for b in range(tile_bits))
        at = lead + (slice(None),) * (rank - tile_bits)
        if j == 0:
            for c in range(2):
                wide = rows[m][c][at].astype(jnp.float32).reshape(128, splits[c])
                xs[m][c][...] = wide.astype(jnp.bfloat16)
        hidden = []
        for weights in (gate_v, up_v):
            value = 0.0
            for c in range(2):
                value = value + dot_t(xs[m][c][...], weights[j, :, starts[c] : starts[c] + splits[c]])
            hidden.append(value)
        g, u = hidden
        active = ((u + 1.0) * g * jax.nn.sigmoid(1.702 * g)).astype(jnp.bfloat16)
        for c in range(2):
            part = jnp.dot(
                active, down_v[j, :, starts[c] : starts[c] + splits[c]], preferred_element_type=jnp.float32
            )
            if j:
                part = outs[m][c][...] + part
            if j < entries - 1:
                outs[m][c][...] = part
                continue
            wide_gates = gates_v[m][at].reshape(128, LANES)
            column = lax.broadcasted_iota(jnp.int32, (128, LANES), 1)
            gate = jnp.sum(jnp.where(column == expert, wide_gates, 0.0), axis=1, keepdims=True)
            part = jnp.where(gate > 0.0, part * gate, 0.0)
            accs[m][c][at] = part.reshape((2,) * (rank - tile_bits) + (8, splits[c]))

    group_bits = group.bit_length() - 1
    half = turns // 2

    def chain(m):
        attend_range(m, 0, half)
        yield "attention"
        attend_range(m, half, turns)
        if m == 0:
            for load in loads[1:]:
                load.start()
            pl.semaphore_wait(barrier, len(masks))
        swaps = []
        for j in range(1, group):
            partner = flip(me, j)
            swap = pltpu.make_async_remote_copy(
                src_ref=heads_v.at[partner % group, m],
                dst_ref=block_v.at[j, m],
                send_sem=swap_sem.at[m, 0, j],
                recv_sem=swap_sem.at[m, 1, j],
                device_id={"req": partner},
                device_id_type=MESH,
            )
            swap.start()
            swaps.append(swap)
        block_v[0, m] = heads_v[mine, m]
        yield "swap"
        for swap in swaps:
            swap.wait()
        if m == 0:
            loads[0].wait()
        for place in range(n):
            mask = sum(((place >> (levels - 1 - d)) & 1) << d for d in range(levels))
            dest = flip(me, mask)
            slot = exclusive(dest // subs % group, mine, group_bits)
            lhs_v[m, place] = block_v[slot, m, dest % subs]
        lhs = lhs_v[m].reshape(n * 8, width).astype(jnp.bfloat16)
        for c in range(2):
            part = dot_t(lhs, o_v[starts[c] : starts[c] + splits[c], :])
            accs[m][c][...] = part.reshape(accs[m][c].shape)
        copies = {}
        for level in range(levels):
            scatter_step(m, 0, level, copies)
            yield "reduce"
        norm_rows(m, scatter_end(m, 0, copies))
        copies = {}
        for level in reversed(range(levels)):
            gather_step(m, level, copies)
            yield "gather"
        for c in range(3):
            copies[0, c].wait_recv()
        for copy in copies.values():
            copy.wait_send()
        if m == 0:
            for load in loads[1:]:
                load.wait()
        copies = {}
        for tile in range(tiles):
            for j in range(entries):
                expert_entry(m, tile, j)
                if (tile, j) == (tiles - 1, entries - 1):
                    scatter_step(m, 1, 0, copies)
                yield "expert"
        for level in range(1, levels):
            scatter_step(m, 1, level, copies)
            yield "combine"
        mixture = scatter_end(m, 1, copies)
        for c in range(2):
            cols = slice(starts[c], starts[c] + splits[c])
            lay_ref[m, :, cols] = (wide_v[m, :, cols] + mixture[c]).astype(jnp.bfloat16)
        yield "end"

    units = tiles * entries
    order = [0, 0, 0, 1, 0, 1, 0, 1]
    order += [0, 1] * (levels - 3)
    order += [0, 1] * levels
    order += [0, 1] + [0] * (units // 2) + [1] + [0] * (units - 1 - units // 2) + [1, 0] * levels
    length = 2 + levels + levels + units + levels - 1 + 1
    chains = [chain(m) for m in range(batches)]
    taken = [0] * batches
    for m in order + [0] * length + [1] * length:
        if taken[m] < length:
            next(chains[m])
            taken[m] += 1


def shards(queries, new_kv, cache, lengths, residual, o_proj, router, w_gate, w_up, w_down, routes):
    n = lax.axis_size("req")
    levels = n.bit_length() - 1
    batches, local, q_cols = queries.shape
    depth = residual.shape[2]
    own_rows = residual.shape[1]
    width = o_proj.shape[0]
    group = q_cols // width
    subs = local // own_rows
    heads = q_cols // HD
    per_expert = max(1, n * w_gate.shape[0] // router.shape[1])
    cut = (depth // 2 + LANES - 1) // LANES * LANES
    splits = (cut, depth - cut)

    gate_t, up_t = jnp.swapaxes(w_gate, 1, 2), jnp.swapaxes(w_up, 1, 2)
    cube = (2,) * levels
    f32, b16 = jnp.float32, jnp.bfloat16
    vmem = pl.BlockSpec(memory_space=pltpu.VMEM)
    smem = pl.BlockSpec(memory_space=pltpu.SMEM)
    hbm = pl.BlockSpec(memory_space=pl.ANY)

    def pair(dtype):
        return [pltpu.VMEM(cube + (own_rows, s), dtype) for s in splits]

    scratch = [
        pltpu.VMEM(cache.shape, b16),
        pltpu.VMEM(o_proj.shape[::-1], b16),
        pltpu.VMEM(gate_t.shape, b16),
        pltpu.VMEM(up_t.shape, b16),
        pltpu.VMEM(w_down.shape, b16),
        pltpu.VMEM((16 * heads, LANES), f32),
        pltpu.VMEM((16 * heads, LANES), f32),
        pltpu.VMEM((group, batches, subs, own_rows, width), f32),
        pltpu.VMEM((group, batches, subs, own_rows, width), f32),
        pltpu.VMEM((batches, n, own_rows, width), f32),
        pltpu.VMEM((batches, own_rows, depth), f32),
        *(pair(f32) * batches),
        *(pair(b16) * batches),
        *(pair(b16) * (2 * batches)),
        *(pair(b16) * batches),
        *([pltpu.VMEM(cube + (own_rows, LANES), f32)] * batches),
        *([pltpu.VMEM((128, s), b16) for s in splits] * batches),
        *([pltpu.VMEM((128, s), f32) for s in splits] * batches),
        pltpu.SemaphoreType.DMA((batches, subs // 2)),
        pltpu.SemaphoreType.DMA((4,)),
        pltpu.SemaphoreType.DMA((batches, 2, group)),
        pltpu.SemaphoreType.DMA((batches, 2, 2, levels, 2)),
        pltpu.SemaphoreType.DMA((batches, 2, levels, 3)),
    ]
    out = jax.ShapeDtypeStruct(residual.shape, b16)
    return pl.pallas_call(
        functools.partial(layer_kernel, (n, levels, group, width, subs, splits, per_expert, batches)),
        out_shape=(out, out),
        in_specs=[vmem, vmem, smem, hbm, vmem, hbm, vmem, hbm, hbm, hbm, vmem],
        out_specs=(vmem, vmem),
        scratch_shapes=scratch,
        compiler_params=pltpu.CompilerParams(
            collective_id=0, has_side_effects=True, vmem_limit_bytes=67043328
        ),
        name="moe_layer",
    )(
        queries, new_kv, lengths, cache, residual, o_proj.T, router.T, gate_t, up_t, w_down,
        jnp.swapaxes(routes, 1, 2),
    )


def solution(mesh):
    placed = (
        P(None, ("groups", "req"), None),
        P(None, ("groups", "req"), None),
        P(None, ("groups", "req"), None, None),
        P(None, "groups"),
        P(None, ("groups", "req"), None),
        P("req", None),
        P(),
        P("req", None, None),
        P("req", None, None),
        P("req", None, None),
        P(None, ("groups", "req"), None),
    )
    if tuple(mesh.axis_names) != ("groups", "req"):
        raise ValueError("mesh axes")
    return jax.shard_map(
        shards,
        mesh=mesh,
        in_specs=placed,
        out_specs=(P(None, ("groups", "req"), None), P(None, ("groups", "req"), None)),
        check_vma=False,
    )
```

time: 82.3 us -> 75.2 us (0.914)
  Pallas kernels: 78.4 us -> 71.3 us
    pallas_call x1, Pallas kernels: 78.4 us -> 71.3 us  [shards(): pl.pallas_call(functools.partial(layer_kernel, (n, levels, group, width,...]
where the time goes in v3:
time: 75.2 us; the launch traced here: 75 us
  Pallas kernels  71.3 us (95%)
  local copies, waits for them, and re-layouts  3.07 us (4%)
    pallas_call x1, Pallas kernels, shards(): pl.pallas_call(functools.partial(layer_kernel, (n, levels, group, width,...  71.3 us
    unnamed x2, local copies, waits for them, and re-layouts  3.07 us

profile of v3, /device:TPU:0, one launch (start us, length us, event | category | flops | bytes accessed | tf_op | source)
XLA Modules:
  0.0 75.0 jit_solution(9149713348549521499)
XLA Ops:
  0.6 71.3 %moe_layer.1 = (bf16[2,8,2880]{2,1,0:T(8,128)(2,1)}, bf16[2,8,2880]{2,1,0:T(8,128)(2,1)}) custom-call(bf16[2,64,512]{2,1,0:T(8,128)(2,1)} %q_ref.1, bf16[2,64,128]{2,1,0:T(8,128)(2,1)} %nk_ref.1, s32[2,128]{1,0:T(2,128)} %len_ref.1, bf16[2,64,128,128]{3,2,1,0:T(8,128)(2,1)} %cache_ref.1, bf16[2,8,2880]{2,1,0:T(8,128)(2,1)} %res_ref.1, ...), custom_call_target="tpu_custom_call" | custom-call | tf_op jit(solution)/shard_map/moe_layer/pallas_call | solution.py:405
  72.0 1.5 %copy.15 = bf16[2,8,2880]{2,1,0:T(8,128)(2,1)} copy(bf16[2,8,2880]{2,1,0:T(8,128)(2,1)} %get-tuple-element.4) | data formatting | bytes 184320
  73.5 1.5 %copy.16 = bf16[2,8,2880]{2,1,0:T(8,128)(2,1)} copy(bf16[2,8,2880]{2,1,0:T(8,128)(2,1)} %get-tuple-element.5) | data formatting | bytes 184320

commit v4 on v3

--- a/solution.py
+++ b/solution.py
@@ -156,15 +156,15 @@
         return tuple(index)
 
     def scatter_step(m, phase, level, copies):
+        arrived = lambda c, at: tuple(1 if d == orders[c][level - 1] else i for d, i in enumerate(at))
         for c in range(2):
             order, acc, landing = orders[c], accs[m][c], landings[m][phase][c]
+            out = region(order, level, 1)
+            value = acc[out]
             if level:
                 copies[level - 1, c].wait_recv()
-                done = region(order, level - 1, 1)
-                kept = region(order, level - 1, 0)
-                acc[kept] = acc[kept] + landing[done].astype(jnp.float32)
-            out = region(order, level, 1)
-            sends[m][c][out] = acc[out].astype(jnp.bfloat16)
+                value = value + landing[arrived(c, out)].astype(jnp.float32)
+            sends[m][c][out] = value.astype(jnp.bfloat16)
             copies[level, c] = pltpu.make_async_remote_copy(
                 src_ref=sends[m][c].at[out],
                 dst_ref=landing.at[out],
@@ -174,6 +174,11 @@
                 device_id_type=MESH,
             )
             copies[level, c].start()
+        if level:
+            for c in range(2):
+                kept = region(orders[c], level, 0)
+                value = landings[m][phase][c][arrived(c, kept)].astype(jnp.float32)
+                accs[m][c][kept] = accs[m][c][kept] + value
 
     def scatter_end(m, phase, copies):
         total = []

time: 75.2 us -> 75.1 us (level)
  no operation moved by 1% of the time
where the time goes in v4:
time: 75.1 us; the launch traced here: 74.9 us
  Pallas kernels  71.2 us (95%)
  local copies, waits for them, and re-layouts  3.07 us (4%)
    pallas_call x1, Pallas kernels, shards(): pl.pallas_call(functools.partial(layer_kernel, (n, levels, group, width,...  71.2 us
    unnamed x2, local copies, waits for them, and re-layouts  3.07 us

profile of v4, /device:TPU:0, one launch (start us, length us, event | category | flops | bytes accessed | tf_op | source)
XLA Modules:
  0.0 74.9 jit_solution(7916338570309960630)
XLA Ops:
  0.6 71.2 %moe_layer.1 = (bf16[2,8,2880]{2,1,0:T(8,128)(2,1)}, bf16[2,8,2880]{2,1,0:T(8,128)(2,1)}) custom-call(bf16[2,64,512]{2,1,0:T(8,128)(2,1)} %q_ref.1, bf16[2,64,128]{2,1,0:T(8,128)(2,1)} %nk_ref.1, s32[2,128]{1,0:T(2,128)} %len_ref.1, bf16[2,64,128,128]{3,2,1,0:T(8,128)(2,1)} %cache_ref.1, bf16[2,8,2880]{2,1,0:T(8,128)(2,1)} %res_ref.1, ...), custom_call_target="tpu_custom_call" | custom-call | tf_op jit(solution)/shard_map/moe_layer/pallas_call | solution.py:410
  71.8 1.5 %copy.15 = bf16[2,8,2880]{2,1,0:T(8,128)(2,1)} copy(bf16[2,8,2880]{2,1,0:T(8,128)(2,1)} %get-tuple-element.4) | data formatting | bytes 184320
  73.3 1.5 %copy.16 = bf16[2,8,2880]{2,1,0:T(8,128)(2,1)} copy(bf16[2,8,2880]{2,1,0:T(8,128)(2,1)} %get-tuple-element.5) | data formatting | bytes 184320
